TPU v7x, 256 devices: a whole 4x4x8 slice. The times are simulated.
256 devices in a mesh: net: 32 (over x, z), scen: 8 (over y, core).
Axes of the slice: x: 4, y: 4, z: 8, core: 2. Of those that a mesh axis runs over, the one named last changes fastest.
Arguments:
- arc_flows: float32 [256, 262144], P('scen', 'net'), may hold values from 0 to 1
- node_duals: float32 [256, 65536], P('scen', 'net'), may hold values from -6 to 6
- demand: float32 [256, 65536], P('scen', 'net'), may hold values from -6 to 6
- excess: float32 [256], P('scen'), may hold values from 0 to 0.5
- risk_duals: float32 [256], P('scen'), may hold values from 0.2 to 6
- threshold: float32 [1], replicated, may hold values from -2.5 to -1.5
- arc_costs: float32 [262144], P('net'), may hold values from 0.05 to 0.75
- local_blocks: bfloat16 [2048, 4, 128, 128], P('net'), may hold values from -0.125 to 0.125
- head_blocks: bfloat16 [2048, 128, 128], P('net'), may hold values from -0.125 to 0.125
- local_index: int32 [2048, 4], P('net'), may hold values from 0 to 15
- head_index: int32 [2048], P('net'), may hold values from 0 to 511, as said below
Outputs:
- flows_next: float32 [256, 262144], P('scen', 'net')
- duals_next: float32 [256, 65536], P('scen', 'net')
- excess_next: float32 [256], P('scen')
- risk_next: float32 [256], P('scen')
- threshold_next: float32 [1], replicated
Inputs may be any that keep to these rules, and one draw needn't show every extreme that they name: Among the arc blocks of one device, at most 4 have their head node block on any one device of net (head_index // 16 names the device), and in every device's arc blocks some device of net is named exactly 4 times.
All inputs are finite; a program needn't handle non-finite values.
Results may differ from a plain program's by a relative error of at most 0.0021.
Values may be sent and summed in bfloat16 or wider, within the bound.
A program may use at most 128 MiB of HBM per device.

v0:
```python
import jax
import jax.numpy as jnp
from jax import lax
from jax.sharding import PartitionSpec as P

ROUNDS = 3
primal_step = 0.5
dual_step = 0.5
risk_step = 1.0
tail_weight = 2.0


def per_device(
    arc_flows,
    node_duals,
    demand,
    excess,
    risk_duals,
    threshold,
    arc_costs,
    local_blocks,
    head_blocks,
    local_index,
    head_index,
):
    block_rows = local_blocks.shape[-1]
    scen_rows = arc_flows.shape[0]
    arc_blks = head_index.shape[0]
    node_blks = node_duals.shape[1] // block_rows
    touches = local_index.shape[1]
    net_size = lax.axis_size("net")
    scen_size = lax.axis_size("scen")
    slot_cap = max(2, (2 * arc_blks + net_size - 1) // net_size)
    slot_count = net_size * slot_cap
    arc_total = arc_flows.shape[1] * net_size
    scen_total = scen_rows * scen_size
    select_prec = lax.Precision.HIGH
    peer_dev = head_index // node_blks
    target = head_index % node_blks
    peer_hot = (peer_dev[:, None] == jnp.arange(net_size, dtype=jnp.int32)[None, :]).astype(
        jnp.int32
    )
    earlier = jnp.cumsum(peer_hot, axis=0) - peer_hot
    slot_rank = jnp.sum(earlier * peer_hot, axis=1)
    slot_ids = peer_dev * slot_cap + slot_rank
    slot_hot = slot_ids[:, None] == jnp.arange(slot_count, dtype=jnp.int32)[None, :]
    arc_ids = jnp.arange(arc_blks, dtype=jnp.int32)
    slot_arc = jnp.max(jnp.where(slot_hot, arc_ids[:, None], -1), axis=0)
    slot_filled = slot_arc >= 0
    slot_source = jnp.maximum(slot_arc, 0)
    wanted = jnp.max(jnp.where(slot_hot, target[:, None], -1), axis=0).reshape(net_size, slot_cap)
    asked = lax.all_to_all(wanted, "net", split_axis=0, concat_axis=0, tiled=True)
    asked_hot = asked.reshape(-1)[:, None] == jnp.arange(node_blks, dtype=jnp.int32)[None, :]
    local_hot = local_index[:, :, None] == jnp.arange(node_blks, dtype=jnp.int32)[None, None, :]
    asked_wide = asked_hot.astype(jnp.float32)
    local_wide = local_hot.astype(jnp.float32)
    local_half = local_hot.astype(jnp.bfloat16)
    flow_now = arc_flows
    dual_now = node_duals
    level = threshold
    excess_now = excess
    risk_now = risk_duals
    for iteration in range(ROUNDS):
        dual_panel = dual_now.astype(jnp.bfloat16)
        dual_grid = dual_panel.reshape(scen_rows, node_blks, block_rows)
        gathered = lax.all_gather(dual_panel, "net", axis=1, tiled=True)
        head_rows = jnp.take(gathered.reshape(scen_rows, -1, block_rows), head_index, axis=1)
        pull_summed = jnp.einsum(
            "sjn,jmn->sjm", head_rows, head_blocks, preferred_element_type=jnp.float32
        )
        for touched in range(touches):
            local_rows = jnp.einsum(
                "sbn,jb->sjn", dual_grid, local_half[:, touched], preferred_element_type=jnp.float32
            ).astype(jnp.bfloat16)
            pull_summed = pull_summed + jnp.einsum(
                "sjn,jmn->sjm",
                local_rows,
                local_blocks[:, touched],
                preferred_element_type=jnp.float32,
            )
        pulled = pull_summed.reshape(scen_rows, arc_blks * block_rows)
        risk_mine = risk_now
        mean_risk = lax.psum(jnp.sum(risk_now), "scen") / scen_total
        flows_new = jnp.maximum(
            flow_now - primal_step * (risk_mine[:, None] * arc_costs[None, :] - pulled), 0.0
        )
        level_new = level - primal_step * (1.0 - mean_risk)
        flows_bar = 2.0 * flows_new - flow_now
        level_bar = 2.0 * level_new - level
        partial_value = jnp.sum(arc_costs[None, :] * flows_bar, axis=1) / arc_total
        excess_new = jnp.maximum(excess_now - primal_step * (tail_weight - risk_now), 0.0)
        excess_bar = 2.0 * excess_new - excess_now
        losses = lax.psum(partial_value, "net")
        risk_now = jnp.maximum(risk_now + risk_step * (losses - excess_bar - level_bar), 0.0)
        excess_now = excess_new
        flow_grid = flows_bar.astype(jnp.bfloat16).reshape(scen_rows, arc_blks, block_rows)
        own_terms = jnp.einsum(
            "sjm,jmn->sjn", flow_grid, head_blocks, preferred_element_type=jnp.float32
        )
        term_pack = jnp.where(
            slot_filled[None, :, None], jnp.take(own_terms, slot_source, axis=1), 0.0
        )
        arrived = lax.all_to_all(
            term_pack.reshape(scen_rows, net_size, slot_cap, block_rows),
            "net",
            split_axis=1,
            concat_axis=1,
            tiled=True,
        )
        head_terms = arrived.reshape(scen_rows, slot_count, block_rows)
        summed = jnp.einsum("sqn,qb->sbn", head_terms, asked_wide, precision=select_prec)
        local_terms = jnp.einsum(
            "sjm,jkmn->sjkn", flow_grid, local_blocks, preferred_element_type=jnp.float32
        )
        summed = summed + jnp.einsum(
            "sjkn,jkb->sbn", local_terms, local_wide, precision=select_prec
        )
        dual_now = dual_now + dual_step * (
            demand - summed.reshape(scen_rows, node_blks * block_rows)
        )
        flow_now = flows_new
        level = level_new
    return (flow_now, dual_now, excess_now, risk_now, level)


def solution(mesh):
    placed = (
        P("scen", "net"),
        P("scen", "net"),
        P("scen", "net"),
        P("scen"),
        P("scen"),
        P(),
        P("net"),
        P("net", None, None, None),
        P("net", None, None),
        P("net", None),
        P("net"),
    )
    return jax.shard_map(
        per_device,
        mesh=mesh,
        in_specs=placed,
        out_specs=(P("scen", "net"), P("scen", "net"), P("scen"), P("scen"), P()),
        check_vma=False,
    )
```

profile of v0, /device:TPU:0, one launch (start us, length us, event | category | flops | bytes accessed | tf_op | source)
XLA Modules:
  0.0 597.3 jit_solution(4962526115088580452)
XLA Ops:
  10.9 9.6 %all-to-all-start = ((s32[32,1,4]{2,1,0:T(1,128)}), s32[32,1,4]{2,1,0:T(1,128)S(1)}, u32[]{:S(2)}, u32[]{:S(2)}) async-start(s32[32,1,4]{2,1,0:T(1,128)} %bitcast.20), calls=%async_computation | async-start | bytes 32768 | tf_op jit(solution)/shard_map/all_to_all | solution.py:52
  27.9 3.8 fusion.16
  31.7 3.9 fusion.22
  35.6 58.6 %all-gather.4.cloned.1.call-done = bf16[32,65536]{1,0:T(8,128)(2,1)} async-done(((bf16[32,2048]{1,0:T(8,128)(2,1)}), bf16[32,65536]{1,0:T(8,128)(2,1)}) %all-gather.4.cloned.1.call-update) | async-done | bytes 4194320 | tf_op jit(solution)/shard_map/all_gather | solution.py:66
  94.2 4.9 copy_bitcast_fusion.2
  116.7 5.4 all-to-all-start.1
  125.6 4.8 convolution_bitcast_fusion.2
  133.5 36.8 %all-to-all-done.1 = f32[32,32,4,128]{3,0,2,1:T(8,128)} async-done(((f32[32,32,4,128]{3,0,2,1:T(8,128)}), f32[32,32,4,128]{3,0,2,1:T(8,128)}, u32[]{:S(2)}, u32[]{:S(2)}) %all-to-all-start.1) | async-done | bytes 2097184 | tf_op jit(solution)/shard_map/all_to_all | solution.py:103
  175.8 13.0 %psum.43 = f32[]{:T(128)} all-reduce(f32[]{:T(128)} %reduce_sum.64), channel_id=1, replica_groups=mesh['net'=32,'scen'=8] {'scen'}, use_global_device_ids=true, to_apply=%region_3.5 | all-reduce | flops 1 | bytes 8 | tf_op jit(solution)/shard_map/psum | solution.py:83
  190.2 72.1 %psum.42 = f32[32]{0:T(128)S(1)} all-reduce(f32[32]{0:T(128)S(1)} %broadcast_multiply_fusion.2), channel_id=1, replica_groups=mesh['net'=32,'scen'=8] {'net'}, use_global_device_ids=true, to_apply=%region_1.3 | all-reduce | flops 32 | bytes 256 | tf_op jit(solution)/shard_map/psum | solution.py:93
  268.9 3.9 fusion.14
  276.5 4.9 copy_bitcast_fusion.1
  299.0 4.8 all-to-all-start.2
  305.5 4.8 convolution_bitcast_fusion.1
  314.1 26.1 %all-to-all-done.2 = f32[32,32,4,128]{3,0,2,1:T(8,128)} async-done(((f32[32,32,4,128]{3,0,2,1:T(8,128)}), f32[32,32,4,128]{3,0,2,1:T(8,128)}, u32[]{:S(2)}, u32[]{:S(2)}) %all-to-all-start.2) | async-done | bytes 2097184 | tf_op jit(solution)/shard_map/all_to_all | solution.py:103
  345.3 13.1 %psum.45 = f32[]{:T(128)} all-reduce(f32[]{:T(128)} %get-tuple-element.16), channel_id=1, replica_groups=mesh['net'=32,'scen'=8] {'scen'}, use_global_device_ids=true, to_apply=%region_11.14 | all-reduce | flops 1 | bytes 8 | tf_op jit(solution)/shard_map/psum | solution.py:83
  359.1 74.1 %psum.44 = f32[32]{0:T(128)S(1)} all-reduce(f32[32]{0:T(128)S(1)} %broadcast_multiply_fusion.1), channel_id=1, replica_groups=mesh['net'=32,'scen'=8] {'net'}, use_global_device_ids=true, to_apply=%region_9.12 | all-reduce | flops 32 | bytes 256 | tf_op jit(solution)/shard_map/psum | solution.py:93
  436.9 3.8 fusion.6
  440.7 3.9 fusion.12
  448.4 4.9 copy_bitcast_fusion
  471.7 4.8 all-to-all-start.3
  476.4 13.9 %psum.47 = f32[]{:T(128)} all-reduce(f32[]{:T(128)} %get-tuple-element.11), channel_id=1, replica_groups=mesh['net'=32,'scen'=8] {'scen'}, use_global_device_ids=true, to_apply=%region_15.18 | all-reduce | flops 1 | bytes 8 | tf_op jit(solution)/shard_map/psum | solution.py:83
  492.4 83.1 %psum.46 = f32[32]{0:T(128)S(1)} all-reduce(f32[32]{0:T(128)S(1)} %broadcast_multiply_fusion), channel_id=1, replica_groups=mesh['net'=32,'scen'=8] {'net'}, use_global_device_ids=true, to_apply=%region_13.16 | all-reduce | flops 32 | bytes 256 | tf_op jit(solution)/shard_map/psum | solution.py:93
  576.1 4.8 convolution_bitcast_fusion
  (151 shorter events, 114.9 us)
Async XLA Ops:
  7.2 95.6 %copy-start = (bf16[64,128,128]{2,1,0:T(8,128)(2,1)S(1)}, bf16[64,128,128]{2,1,0:T(8,128)(2,1)}, u32[]{:S(2)}) copy-start(bf16[64,128,128]{2,1,0:T(8,128)(2,1)} %param.23) | copy-start | bytes 6291460
  7.2 87.1 %all-gather.4.cloned.1.call-start = ((), (), s32[]{:S(2)}) async-start(), calls=%async_computation.4 | async-start | bytes 4325376 | tf_op jit(solution)/shard_map/all_gather | solution.py:66
  10.9 105.9 %all-to-all-start = ((s32[32,1,4]{2,1,0:T(1,128)}), s32[32,1,4]{2,1,0:T(1,128)S(1)}, u32[]{:S(2)}, u32[]{:S(2)}) async-start(s32[32,1,4]{2,1,0:T(1,128)} %bitcast.20), calls=%async_computation | async-start | bytes 32768 | tf_op jit(solution)/shard_map/all_to_all | solution.py:52
  102.7 2.4 copy-start.11
  102.7 2.5 copy-start.22
  105.2 3.0 copy-start.3
  105.2 3.0 copy-start.25
  105.2 3.0 copy-start.27
  108.8 15.3 %copy-start.1 = (f32[32,8192]{1,0:T(8,128)}, f32[32,8192]{1,0:T(8,128)S(1)}, u32[]{:S(2)}) copy-start(f32[32,8192]{1,0:T(8,128)S(1)} %get-tuple-element.21) | copy-start | bytes 3145732
  116.7 53.5 %all-to-all-start.1 = ((f32[32,32,4,128]{3,0,2,1:T(8,128)}), f32[32,32,4,128]{3,0,2,1:T(8,128)}, u32[]{:S(2)}, u32[]{:S(2)}) async-start(f32[32,32,4,128]{3,0,2,1:T(8,128)} %bitcast.330), calls=%async_computation.1 | async-start | bytes 4194304 | tf_op jit(solution)/shard_map/all_to_all | solution.py:103
  122.2 154.4 %all-gather.6.cloned.1.call-start = ((), (), s32[]{:S(2)}) async-start(), calls=%async_computation.5 | async-start | bytes 4325376 | tf_op jit(solution)/shard_map/all_gather | solution.py:66
  125.5 4.9 copy-start.26
  173.2 89.1 %copy-start.28 = (f32[32]{0:T(128)S(1)}, f32[32]{0:T(128)}, u32[]{:S(2)}) copy-start(f32[32]{0:T(128)} %param.18) | copy-start | bytes 388
  285.0 2.4 copy-start.12
  285.0 2.4 copy-start.23
  287.5 3.0 copy-start.2
  299.0 41.3 %all-to-all-start.2 = ((f32[32,32,4,128]{3,0,2,1:T(8,128)}), f32[32,32,4,128]{3,0,2,1:T(8,128)}, u32[]{:S(2)}, u32[]{:S(2)}) async-start(f32[32,32,4,128]{3,0,2,1:T(8,128)} %bitcast.331), calls=%async_computation.2 | async-start | bytes 4194304 | tf_op jit(solution)/shard_map/all_to_all | solution.py:103
  303.8 144.6 %all-gather.8.cloned.1.call-start = ((), (), s32[]{:S(2)}) async-start(), calls=%async_computation.6 | async-start | bytes 4325376 | tf_op jit(solution)/shard_map/all_gather | solution.py:66
  340.3 3.0 copy-start.24
  456.9 2.4 copy-start.6
  456.9 2.4 copy-start.7
  456.9 2.5 copy-start.8
  456.9 2.5 copy-start.21
  471.7 112.4 %all-to-all-start.3 = ((f32[32,32,4,128]{3,0,2,1:T(8,128)}), f32[32,32,4,128]{3,0,2,1:T(8,128)}, u32[]{:S(2)}, u32[]{:S(2)}) async-start(f32[32,32,4,128]{3,0,2,1:T(8,128)} %bitcast.329), calls=%async_computation.3 | async-start | bytes 4194304 | tf_op jit(solution)/shard_map/all_to_all | solution.py:103
  (12 other events, 15.2 us)
Sparse Core Ops, SparseCore 0:
  11.2 83.0 all-gather.3
  175.4 78.8 all-gather.5
  345.4 77.5 all-gather.7
where the time goes:
time: 606 us; the launch traced here: 597 us
  blocking collectives  269 us (44%)
  waiting for transfers between devices  122 us (20%)
  matrix products  85.9 us (14%)
  local copies, waits for them, and re-layouts  50.6 us (8%)
  other arithmetic  25.8 us (4%)
  starting transfers between devices  25.4 us (4%)
  between operations  18.5 us (3%)
    psum x3, blocking collectives, per_device(): losses = lax.psum(partial_value, 'net')  229 us
    all_to_all x3, waiting for transfers between devices, per_device(): lax.all_to_all(term_pack.reshape(scen_rows, net_size, slot_cap, block_row...  62.9 us
    all_gather x3, waiting for transfers between devices, per_device(): gathered = lax.all_gather(dual_panel, 'net', axis=1, tiled=True)  58.6 us
    dot_general x12, matrix products, per_device(): jnp.einsum('sjn,jmn->sjm', local_rows, local_blocks[:, touched], preferre...  41.3 us
    psum x3, blocking collectives, per_device(): mean_risk = lax.psum(jnp.sum(risk_now), 'scen') / scen_total  40 us
    all_to_all x3, starting transfers between devices, per_device(): lax.all_to_all(term_pack.reshape(scen_rows, net_size, slot_cap, block_row...  15 us
    reshape x3, local copies, waits for them, and re-layouts, per_device(): gathered.reshape(scen_rows, -1, block_rows)  14.6 us
    dot_general x3, matrix products, per_device(): jnp.einsum('sjm,jkmn->sjkn', flow_grid, local_blocks, preferred_element_t...  14.5 us
  transfers between devices with their start and end apart: 7, of which 3 were waited for; matrix products, arithmetic and copies ran while one was open for 17% of the time, Pallas kernels for 0%

commit v1 on v0

--- a/solution.py
+++ b/solution.py
@@ -8,6 +8,13 @@
 dual_step = 0.5
 risk_step = 1.0
 tail_weight = 2.0
+
+
+def trade_parts(array, axis, split, join):
+    count = lax.axis_size(axis)
+    blocks = jnp.stack(jnp.split(array, count, axis=split), axis=0)
+    blocks = lax.all_to_all(blocks, axis, split_axis=0, concat_axis=0)
+    return jnp.concatenate(blocks, axis=join)
 
 
 def per_device(
@@ -100,12 +107,8 @@
         term_pack = jnp.where(
             slot_filled[None, :, None], jnp.take(own_terms, slot_source, axis=1), 0.0
         )
-        arrived = lax.all_to_all(
-            term_pack.reshape(scen_rows, net_size, slot_cap, block_rows),
-            "net",
-            split_axis=1,
-            concat_axis=1,
-            tiled=True,
+        arrived = trade_parts(
+            term_pack.reshape(scen_rows, net_size, slot_cap, block_rows), "net", 1, 1
         )
         head_terms = arrived.reshape(scen_rows, slot_count, block_rows)
         summed = jnp.einsum("sqn,qb->sbn", head_terms, asked_wide, precision=select_prec)

time: 606 us -> 663 us (1.094)
  local copies, waits for them, and re-layouts: 50.6 us -> 111 us
    unnamed x64 -> x157, local copies, waits for them, and re-layouts: 5.36 us -> 63.9 us
    all_to_all x3 -> x0, local copies, waits for them, and re-layouts: 8.87 us -> none  [per_device(): lax.all_to_all(term_pack.reshape(scen_rows, net_size, slot_cap, block_row...]
    reshape x0 -> x3, local copies, waits for them, and re-layouts: none -> 8.87 us  [trade_parts(): return jnp.concatenate(blocks, axis=join)]
  transfers between devices with their start and end apart: 7 -> 7, of which waited for: 3 -> 3; matrix products, arithmetic and copies ran while one was open for 17% -> 18% of each run, Pallas kernels for 0% -> 0%
where the time goes in v1:
time: 663 us; the launch traced here: 655 us
  blocking collectives  269 us (41%)
  waiting for transfers between devices  122 us (18%)
  local copies, waits for them, and re-layouts  111 us (17%)
  matrix products  86 us (13%)
  starting transfers between devices  25.4 us (4%)
  other arithmetic  22.9 us (3%)
  between operations  18.6 us (3%)
    psum x3, blocking collectives, per_device(): losses = lax.psum(partial_value, 'net')  229 us
    unnamed x157, local copies, waits for them, and re-layouts  63.9 us
    all_to_all x3, waiting for transfers between devices, trade_parts(): blocks = lax.all_to_all(blocks, axis, split_axis=0, concat_axis=0)  63 us
    all_gather x3, waiting for transfers between devices, per_device(): gathered = lax.all_gather(dual_panel, 'net', axis=1, tiled=True)  58.6 us
    dot_general x12, matrix products, per_device(): jnp.einsum('sjn,jmn->sjm', local_rows, local_blocks[:, touched], preferre...  41.3 us
    psum x3, blocking collectives, per_device(): mean_risk = lax.psum(jnp.sum(risk_now), 'scen') / scen_total  40 us
    all_to_all x3, starting transfers between devices, trade_parts(): blocks = lax.all_to_all(blocks, axis, split_axis=0, concat_axis=0)  15 us
    reshape x3, local copies, waits for them, and re-layouts, per_device(): gathered.reshape(scen_rows, -1, block_rows)  14.6 us
  transfers between devices with their start and end apart: 7, of which 3 were waited for; matrix products, arithmetic and copies ran while one was open for 18% of the time, Pallas kernels for 0%

profile of v1, /device:TPU:0, one launch (start us, length us, event | category | flops | bytes accessed | tf_op | source)
XLA Modules:
  0.0 655.0 jit_solution(1158202875819392403)
XLA Ops:
  10.9 9.6 %all-to-all-start = ((s32[32,1,4]{2,1,0:T(1,128)}), s32[32,1,4]{2,1,0:T(1,128)S(1)}, u32[]{:S(2)}, u32[]{:S(2)}) async-start(s32[32,1,4]{2,1,0:T(1,128)} %bitcast.20), calls=%async_computation | async-start | bytes 32768 | tf_op jit(solution)/shard_map/all_to_all | solution.py:59
  27.9 3.8 fusion.16
  31.7 3.9 fusion.22
  35.6 58.6 %all-gather.4.cloned.1.call-done = bf16[32,65536]{1,0:T(8,128)(2,1)} async-done(((bf16[32,2048]{1,0:T(8,128)(2,1)}), bf16[32,65536]{1,0:T(8,128)(2,1)}) %all-gather.4.cloned.1.call-update) | async-done | bytes 4194320 | tf_op jit(solution)/shard_map/all_gather | solution.py:73
  94.2 4.9 copy_bitcast_fusion.2
  136.0 5.4 all-to-all-start.1
  144.8 4.8 convolution_bitcast_fusion.2
  152.7 36.8 %all-to-all-done.1 = f32[32,32,1,4,128]{4,1,3,2,0:T(8,128)} async-done(((f32[32,32,1,4,128]{4,1,3,2,0:T(8,128)}), f32[32,32,1,4,128]{4,1,3,2,0:T(8,128)}, u32[]{:S(2)}, u32[]{:S(2)}) %all-to-all-start.1) | async-done | bytes 2097184 | tf_op jit(solution)/shard_map/all_to_all | solution.py:16
  195.1 13.0 %psum.43 = f32[]{:T(128)} all-reduce(f32[]{:T(128)} %reduce_sum.64), channel_id=1, replica_groups=mesh['net'=32,'scen'=8] {'scen'}, use_global_device_ids=true, to_apply=%region_3.5 | all-reduce | flops 1 | bytes 8 | tf_op jit(solution)/shard_map/psum | solution.py:90
  209.4 72.1 %psum.42 = f32[32]{0:T(128)S(1)} all-reduce(f32[32]{0:T(128)S(1)} %broadcast_multiply_fusion.2), channel_id=1, replica_groups=mesh['net'=32,'scen'=8] {'net'}, use_global_device_ids=true, to_apply=%region_1.3 | all-reduce | flops 32 | bytes 256 | tf_op jit(solution)/shard_map/psum | solution.py:100
  288.1 3.9 fusion.14
  295.8 4.9 copy_bitcast_fusion.1
  337.4 4.8 all-to-all-start.2
  343.9 4.8 convolution_bitcast_fusion.1
  352.6 26.2 %all-to-all-done.2 = f32[32,32,1,4,128]{4,1,3,2,0:T(8,128)} async-done(((f32[32,32,1,4,128]{4,1,3,2,0:T(8,128)}), f32[32,32,1,4,128]{4,1,3,2,0:T(8,128)}, u32[]{:S(2)}, u32[]{:S(2)}) %all-to-all-start.2) | async-done | bytes 2097184 | tf_op jit(solution)/shard_map/all_to_all | solution.py:16
  383.8 13.1 %psum.45 = f32[]{:T(128)} all-reduce(f32[]{:T(128)} %get-tuple-element.16), channel_id=1, replica_groups=mesh['net'=32,'scen'=8] {'scen'}, use_global_device_ids=true, to_apply=%region_11.14 | all-reduce | flops 1 | bytes 8 | tf_op jit(solution)/shard_map/psum | solution.py:90
  397.5 74.1 %psum.44 = f32[32]{0:T(128)S(1)} all-reduce(f32[32]{0:T(128)S(1)} %broadcast_multiply_fusion.1), channel_id=1, replica_groups=mesh['net'=32,'scen'=8] {'net'}, use_global_device_ids=true, to_apply=%region_9.12 | all-reduce | flops 32 | bytes 256 | tf_op jit(solution)/shard_map/psum | solution.py:100
  475.4 3.8 fusion.6
  479.2 3.9 fusion.12
  486.9 4.9 copy_bitcast_fusion
  529.4 4.8 all-to-all-start.3
  534.1 13.9 %psum.47 = f32[]{:T(128)} all-reduce(f32[]{:T(128)} %get-tuple-element.11), channel_id=1, replica_groups=mesh['net'=32,'scen'=8] {'scen'}, use_global_device_ids=true, to_apply=%region_15.18 | all-reduce | flops 1 | bytes 8 | tf_op jit(solution)/shard_map/psum | solution.py:90
  550.1 83.1 %psum.46 = f32[32]{0:T(128)S(1)} all-reduce(f32[32]{0:T(128)S(1)} %broadcast_multiply_fusion), channel_id=1, replica_groups=mesh['net'=32,'scen'=8] {'net'}, use_global_device_ids=true, to_apply=%region_13.16 | all-reduce | flops 32 | bytes 256 | tf_op jit(solution)/shard_map/psum | solution.py:100
  633.8 4.8 convolution_bitcast_fusion
  (247 shorter events, 172.5 us)
Async XLA Ops:
  7.2 95.6 %copy-start = (bf16[64,128,128]{2,1,0:T(8,128)(2,1)S(1)}, bf16[64,128,128]{2,1,0:T(8,128)(2,1)}, u32[]{:S(2)}) copy-start(bf16[64,128,128]{2,1,0:T(8,128)(2,1)} %param.23) | copy-start | bytes 6291460
  7.2 87.1 %all-gather.4.cloned.1.call-start = ((), (), s32[]{:S(2)}) async-start(), calls=%async_computation.4 | async-start | bytes 4325376 | tf_op jit(solution)/shard_map/all_gather | solution.py:73
  10.9 125.1 %all-to-all-start = ((s32[32,1,4]{2,1,0:T(1,128)}), s32[32,1,4]{2,1,0:T(1,128)S(1)}, u32[]{:S(2)}, u32[]{:S(2)}) async-start(s32[32,1,4]{2,1,0:T(1,128)} %bitcast.20), calls=%async_computation | async-start | bytes 32768 | tf_op jit(solution)/shard_map/all_to_all | solution.py:59
  102.7 2.4 copy-start.11
  102.7 2.5 copy-start.22
  105.2 3.0 copy-start.3
  105.2 3.0 copy-start.25
  105.2 3.0 copy-start.27
  108.8 34.5 %copy-start.1 = (f32[32,8192]{1,0:T(8,128)}, f32[32,8192]{1,0:T(8,128)S(1)}, u32[]{:S(2)}) copy-start(f32[32,8192]{1,0:T(8,128)S(1)} %get-tuple-element.21) | copy-start | bytes 3145732
  136.0 53.5 %all-to-all-start.1 = ((f32[32,32,1,4,128]{4,1,3,2,0:T(8,128)}), f32[32,32,1,4,128]{4,1,3,2,0:T(8,128)}, u32[]{:S(2)}, u32[]{:S(2)}) async-start(f32[32,32,1,4,128]{4,1,3,2,0:T(8,128)} %constant_dynamic-update-slice_fusion), calls=%async_computation.1 | async-start | bytes 4194304 | tf_op jit(solution)/shard_map/all_to_all | solution.py:16
  141.4 154.3 %all-gather.6.cloned.1.call-start = ((), (), s32[]{:S(2)}) async-start(), calls=%async_computation.5 | async-start | bytes 4325376 | tf_op jit(solution)/shard_map/all_gather | solution.py:73
  144.8 4.9 copy-start.26
  192.5 89.1 %copy-start.28 = (f32[32]{0:T(128)S(1)}, f32[32]{0:T(128)}, u32[]{:S(2)}) copy-start(f32[32]{0:T(128)} %param.18) | copy-start | bytes 388
  304.2 2.4 copy-start.12
  304.2 2.4 copy-start.23
  306.7 3.0 copy-start.2
  337.4 41.3 %all-to-all-start.2 = ((f32[32,32,1,4,128]{4,1,3,2,0:T(8,128)}), f32[32,32,1,4,128]{4,1,3,2,0:T(8,128)}, u32[]{:S(2)}, u32[]{:S(2)}) async-start(f32[32,32,1,4,128]{4,1,3,2,0:T(8,128)} %constant_dynamic-update-slice_fusion.32), calls=%async_computation.2 | async-start | bytes 4194304 | tf_op jit(solution)/shard_map/all_to_all | solution.py:16
  342.2 144.7 %all-gather.8.cloned.1.call-start = ((), (), s32[]{:S(2)}) async-start(), calls=%async_computation.6 | async-start | bytes 4325376 | tf_op jit(solution)/shard_map/all_gather | solution.py:73
  378.7 3.0 copy-start.24
  495.3 2.4 copy-start.6
  495.3 2.4 copy-start.7
  495.3 2.5 copy-start.8
  495.3 2.5 copy-start.21
  529.4 112.4 %all-to-all-start.3 = ((f32[32,32,1,4,128]{4,1,3,2,0:T(8,128)}), f32[32,32,1,4,128]{4,1,3,2,0:T(8,128)}, u32[]{:S(2)}, u32[]{:S(2)}) async-start(f32[32,32,1,4,128]{4,1,3,2,0:T(8,128)} %constant_dynamic-update-slice_fusion.64), calls=%async_computation.3 | async-start | bytes 4194304 | tf_op jit(solution)/shard_map/all_to_all | solution.py:16
  (12 other events, 15.2 us)
Sparse Core Ops, SparseCore 0:
  11.2 83.0 all-gather.3
  194.6 78.8 all-gather.5
  383.9 77.5 all-gather.7
